TPU v7x, 256 devices: a whole 4x4x8 slice. The times are simulated.
256 devices in a mesh: dp: 4 (over y_hi, core), seq: 8 (over z), head: 8 (over x, y_lo).
Axes of the slice: x: 4, y: 4 (y_hi: 2, y_lo: 2; y = y_hi * 2 + y_lo), z: 8, core: 2. Of those that a mesh axis runs over, the one named last changes fastest.
Arguments:
- tokens: bfloat16 [4, 8192, 512], P('dp', ('seq', 'head')), may hold values from -800 to 800
- bin_ids: int32 [4, 8192], P('dp'), may hold values from 0 to 127, never falling along the last dimension, each value on 1 to 256 neighbouring positions
- pattern: int32 [4, 64, 9], P('dp'), may hold values from 0 to 63, as said below
- w_qkv: bfloat16 [512, 1536], replicated, may hold values from -3.2 to 3.2
- w_out: bfloat16 [512, 512], replicated, may hold values from -5 to 5
- head_bias: float32 [8], replicated, may hold values from -3 to 400
- grad_output: bfloat16 [4, 8192, 512], P('dp', ('seq', 'head')), may hold values from -6 to 6
Outputs:
- output: bfloat16 [4, 8192, 512], P('dp', ('seq', 'head'))
- grad_tokens: bfloat16 [4, 8192, 512], P('dp', ('seq', 'head'))
- grad_w_qkv: float32 [512, 1536], P(None, 'head')
- grad_w_out: float32 [512, 512], P('head')
Inputs may be any that keep to these rules, and one draw needn't show every extreme that they name: `pattern`: row i of sequence b lists (i + o) mod 64 for the 9 offsets o of sequence b, in the same order in every row: 0, 1, -1, then distinct a from 2 to 31, then their negatives. So block J is in row I exactly when I is in row J. `bin_ids`: bin numbers never fall along a sequence.
All inputs are finite; a program needn't handle non-finite values.
Results may differ from a plain program's by a relative error of at most 0.01.
Values may be sent and summed in bfloat16 or wider, within the bound.
A program may use at most 64 MiB of HBM per device.

v0:
```python
import math
import jax
import jax.numpy as jnp
from jax import lax
from jax.sharding import PartitionSpec as P

D = 512
HEADS = 8
HD = 64
BLK = 128
NNZ = 9
EPSILON = 1e-05


def normalize(token_rows):
    widened = token_rows.astype(jnp.float32)
    spread = jnp.sqrt(jnp.mean(widened * widened, axis=-1, keepdims=True) + EPSILON)
    return (widened / spread, spread)


def query_scores(query_blk, key_blk, bin_query, bin_key, bias_local, factor):
    raw_scores = jnp.einsum(
        "gqhe,gnkhe->ghqnk", query_blk, key_blk, preferred_element_type=jnp.float32
    )
    same_bin = (bin_query[:, None, :, None, None] == bin_key[:, None, None, :, :]).astype(
        jnp.float32
    )
    scores = raw_scores * factor + bias_local[None, :, None, None, None] * same_bin
    return scores.reshape(scores.shape[0], scores.shape[1], scores.shape[2], -1)


def body(tokens, bin_ids, pattern, w_qkv, w_out, head_bias, grad_output):
    tok_rows = tokens.shape[1]
    head_parts = lax.axis_size("head")
    local_heads = HEADS // head_parts
    seq_rows = tok_rows * head_parts
    seq_length = bin_ids.shape[1]
    blocks_all = seq_length // BLK
    local_blocks = seq_rows // BLK
    group_size = math.gcd(local_blocks, 4)
    group_count = local_blocks // group_size
    factor = 1.0 / math.sqrt(HD)
    seq_pos = lax.axis_index("seq")
    head_pos = lax.axis_index("head")
    first_block = seq_pos * local_blocks
    key_lists = lax.dynamic_slice_in_dim(pattern[0], first_block, local_blocks, 0)
    bin_table = bin_ids[0].reshape(blocks_all, BLK)
    bin_local = lax.dynamic_slice_in_dim(bin_table, first_block, local_blocks, 0)
    bias_local = lax.dynamic_slice_in_dim(head_bias, head_pos * local_heads, local_heads, 0)

    def grouped(array):
        return array.reshape((group_count, group_size) + array.shape[1:])

    normed, spread = normalize(tokens[0])
    hidden = normed.astype(jnp.bfloat16)
    packed = jnp.dot(hidden, w_qkv, preferred_element_type=jnp.float32).astype(jnp.bfloat16)
    packed = packed.reshape(tok_rows, HEADS, 3 * HD)
    packed_heads = lax.all_to_all(packed, "head", split_axis=1, concat_axis=0, tiled=True)
    queries = packed_heads[:, :, :HD]
    pair_local = packed_heads[:, :, HD:]
    pair_all = lax.all_gather(pair_local, "seq", axis=0, tiled=True)
    pair_table = pair_all.reshape(blocks_all, BLK, local_heads, 2 * HD)
    query_blocks = queries.reshape(local_blocks, BLK, local_heads, HD)

    def forward_group(entries):
        query_blk, key_rows, bin_query = entries
        pair_blk = jnp.take(pair_table, key_rows, axis=0)
        bin_key = jnp.take(bin_table, key_rows, axis=0)
        scores = query_scores(query_blk, pair_blk[..., :HD], bin_query, bin_key, bias_local, factor)
        row_max = jnp.max(scores, axis=-1, keepdims=True)
        log_total = row_max + jnp.log(jnp.sum(jnp.exp(scores - row_max), axis=-1, keepdims=True))
        probs = jnp.exp(scores - log_total).astype(jnp.bfloat16)
        value_flat = pair_blk[..., HD:].reshape(group_size, NNZ * BLK, local_heads, HD)
        attended = jnp.einsum(
            "ghqm,gmhe->gqhe", probs, value_flat, preferred_element_type=jnp.float32
        )
        return (attended.astype(jnp.bfloat16), log_total[..., 0])

    attended, log_blocks = lax.map(
        forward_group, (grouped(query_blocks), grouped(key_lists), grouped(bin_local))
    )
    attended_heads = attended.reshape(seq_rows, local_heads, HD)
    log_blocks = log_blocks.reshape(local_blocks, local_heads, BLK)
    attended_tok = lax.all_to_all(
        attended_heads, "head", split_axis=0, concat_axis=1, tiled=True
    ).reshape(tok_rows, D)
    result = jnp.dot(attended_tok, w_out, preferred_element_type=jnp.float32).astype(jnp.bfloat16)
    grad_rows = grad_output[0]
    grad_att = jnp.dot(grad_rows, w_out.T, preferred_element_type=jnp.float32).astype(jnp.bfloat16)
    grad_heads = lax.all_to_all(
        grad_att.reshape(tok_rows, HEADS, HD), "head", split_axis=1, concat_axis=0, tiled=True
    )
    delta_rows = jnp.sum(
        grad_heads.astype(jnp.float32) * attended_heads.astype(jnp.float32), axis=-1
    )
    delta_blocks = delta_rows.reshape(local_blocks, BLK, local_heads).swapaxes(1, 2)
    grad_blocks = grad_heads.reshape(local_blocks, BLK, local_heads, HD)

    def query_core(entries):
        query_blk, grad_blk, log_blk, delta_blk, key_rows, bin_query = entries
        pair_blk = jnp.take(pair_table, key_rows, axis=0)
        bin_key = jnp.take(bin_table, key_rows, axis=0)
        scores = query_scores(query_blk, pair_blk[..., :HD], bin_query, bin_key, bias_local, factor)
        probs = jnp.exp(scores - log_blk[..., None])
        value_flat = pair_blk[..., HD:].reshape(group_size, NNZ * BLK, local_heads, HD)
        key_flat = pair_blk[..., :HD].reshape(group_size, NNZ * BLK, local_heads, HD)
        grad_prob = jnp.einsum(
            "gqhe,gmhe->ghqm", grad_blk, value_flat, preferred_element_type=jnp.float32
        )
        grad_score = (probs * (grad_prob - delta_blk[..., None]) * factor).astype(jnp.bfloat16)
        grad_query = jnp.einsum(
            "ghqm,gmhe->gqhe", grad_score, key_flat, preferred_element_type=jnp.float32
        )
        return (grad_query.astype(jnp.bfloat16), grad_score, probs)

    query_entries = (
        grouped(query_blocks),
        grouped(grad_blocks),
        grouped(log_blocks),
        grouped(delta_blocks),
        grouped(key_lists),
        grouped(bin_local),
    )

    def scatter_step(carried, entries):
        query_blk, grad_blk = (entries[0], entries[1])
        key_rows = entries[4]
        grad_query, grad_score, probs = query_core(entries)
        key_part = jnp.einsum(
            "ghqm,gqhe->gmhe", grad_score, query_blk, preferred_element_type=jnp.float32
        )
        value_part = jnp.einsum(
            "ghqm,gqhe->gmhe",
            probs.astype(jnp.bfloat16),
            grad_blk,
            preferred_element_type=jnp.float32,
        )
        both_parts = jnp.concatenate([key_part, value_part], axis=-1)
        both_parts = both_parts.reshape(group_size * NNZ, BLK, local_heads, 2 * HD)
        carried = carried.at[key_rows.reshape(-1)].add(both_parts)
        return (carried, grad_query)

    empty_sum = jnp.zeros((blocks_all, BLK, local_heads, 2 * HD), jnp.float32)
    pair_sums, grad_queries = lax.scan(scatter_step, empty_sum, query_entries)
    own_pairs = lax.psum_scatter(
        pair_sums.reshape(seq_length, local_heads, 2 * HD), "seq", scatter_dimension=0, tiled=True
    )
    grad_pairs = own_pairs.astype(jnp.bfloat16)
    grad_packed_heads = jnp.concatenate(
        [grad_queries.reshape(seq_rows, local_heads, HD), grad_pairs], axis=-1
    )
    grad_packed = lax.all_to_all(
        grad_packed_heads, "head", split_axis=0, concat_axis=1, tiled=True
    ).reshape(tok_rows, 3 * D)
    grad_hidden = jnp.dot(grad_packed, w_qkv.T, preferred_element_type=jnp.float32)
    inner = jnp.mean(grad_hidden * normed, axis=-1, keepdims=True)
    grad_input = ((grad_hidden - normed * inner) / spread).astype(jnp.bfloat16)
    local_qkv = jnp.einsum("td,tc->dc", hidden, grad_packed, preferred_element_type=jnp.float32)
    local_out = jnp.einsum("td,tc->dc", grad_rows, attended_tok, preferred_element_type=jnp.float32)
    total_qkv, total_out = lax.psum((local_qkv, local_out), ("dp", "seq", "head"))
    own_qkv = lax.dynamic_slice_in_dim(
        total_qkv, head_pos * local_heads * 3 * HD, local_heads * 3 * HD, 1
    )
    own_out = lax.dynamic_slice_in_dim(total_out, head_pos * local_heads * HD, local_heads * HD, 1)
    return (result[None], grad_input[None], own_qkv, own_out.T)


def solution(mesh):
    return jax.shard_map(
        body,
        mesh=mesh,
        in_specs=(
            P("dp", ("seq", "head"), None),
            P("dp", None),
            P("dp", None, None),
            P(),
            P(),
            P(),
            P("dp", ("seq", "head"), None),
        ),
        out_specs=(
            P("dp", ("seq", "head"), None),
            P("dp", ("seq", "head"), None),
            P(None, "head"),
            P("head", None),
        ),
        check_vma=False,
    )
```

profile of v0, /device:TPU:2, one launch (start us, length us, event | category | flops | bytes accessed | tf_op | source)
XLA Modules:
  0.0 558.7 jit_solution(6286347255980764140)
XLA Ops:
  10.6 12.6 %all_to_all.63 = bf16[128,8,192]{0,2,1:T(8,128)(2,1)S(1)} all-to-all(bf16[128,8,192]{0,2,1:T(8,128)(2,1)S(1)} %bitcast.271), channel_id=1, replica_groups=mesh['dp'=4,'seq'=8,'head'=8] {'head'}, dimensions={1} | all-to-all | bytes 786432 | tf_op jit(solution)/shard_map/all_to_all | solution.py:58
  25.1 4.8 all-to-all-start.2
  30.9 36.5 %all-gather.2.cloned.1.call-done = bf16[8192,1,128]{0,2,1:T(8,128)(2,1)} async-done(((bf16[1024,1,128]{0,2,1:T(8,128)(2,1)}), bf16[8192,1,128]{0,2,1:T(8,128)(2,1)}) %all-gather.2.cloned.1.call-update) | async-done | bytes 2097168 | tf_op jit(solution)/shard_map/all_gather | solution.py:61
  67.4 4.1 copy.119
  72.1 40.3 %while.24 = (s32[]{:T(128)}, bf16[2,4,128,1,64]{2,4,1,3,0:T(8,128)(2,1)}, f32[2,4,1,128]{3,1,2,0:T(4,128)}, s32[2,4,9]{2,1,0:T(4,128)S(1)}, bf16[64,128,1,128]{3...) while((s32[]{:T(128)}, ...), condition=%wide.region_4.7_spmd, body=%wide.region_1.6_spmd.sunk | while | flops 156931296 | bytes 39141280 | solution.py:79
  73.5 3.4 gather_fusion
  76.9 1.7 copy.151
  80.7 3.7 fusion.80
  86.2 3.1 copy.153
  89.3 2.3 fusion.81
  93.6 3.4 gather_fusion
  97.0 1.7 copy.151
  100.8 3.7 fusion.80
  106.3 3.1 copy.153
  109.4 2.3 fusion.81
  114.1 2.5 broadcast_in_dim.54
  116.5 86.1 %while.25 = (s32[]{:T(128)}, f32[64,128,1,128]{3,1,0,2:T(8,128)}, bf16[2,4,128,1,64]{2,4,1,3,0:T(8,128)(2,1)}, s32[2,4,9]{2,1,0:T(4,128)S(1)}, bf16[2,4,128,1,64...) while((s32[]{:T(128)}, f32[64,128,1,128]{3,1,0,2:T(8,128)}, ...), condition=%wide.region_8.11_spmd, body=%wide.region_6.10_spmd.sunk | while | flops 385783744 | bytes 64560684 | solution.py:144
  119.2 2.4 gather_fusion.3
  126.9 1.5 reshape.431
  128.3 2.5 copy.158
  130.9 2.1 reshape.432
  133.0 4.2 select_add_fusion.3
  137.2 3.1 copy.155
  140.3 2.5 fusion.94
  144.9 1.6 pad_maximum_fusion.3
  146.5 3.1 copy.157
  149.6 10.0 %scatter_fusion = f32[64,128,128]{2,1,0:T(8,128)} fusion(f32[64,128,128]{2,1,0:T(8,128)} %bitcast.263, s32[36]{0:T(128)S(1)} %copy-done.24, f32[36,128,128]{2,1,0:T(8,128)} %bitcast.257), kind=kCustom, calls=%fused_computation.4.clone.1 | custom fusion | flops 589824 | bytes 7078032 | tf_op jit(solution)/shard_map/while/body/eval_jaxpr/scatter-add | solution.py:140
  162.2 2.4 gather_fusion.3
  169.8 1.5 reshape.431
  171.3 2.5 copy.158
  173.8 2.1 reshape.432
  176.0 4.2 select_add_fusion.3
  180.2 3.1 copy.155
  183.3 2.5 fusion.94
  187.8 1.6 pad_maximum_fusion.3
  189.4 3.1 copy.157
  192.5 10.0 %scatter_fusion = f32[64,128,128]{2,1,0:T(8,128)} fusion(f32[64,128,128]{2,1,0:T(8,128)} %bitcast.263, s32[36]{0:T(128)S(1)} %copy-done.24, f32[36,128,128]{2,1,0:T(8,128)} %bitcast.257), kind=kCustom, calls=%fused_computation.4.clone.1 | custom fusion | flops 589824 | bytes 7078032 | tf_op jit(solution)/shard_map/while/body/eval_jaxpr/scatter-add | solution.py:140
  204.5 2.3 reduce.9
  207.7 5.7 %all-to-all-start.1 = ((bf16[8,2,4096]{2,1,0:T(2,128)(2,1)}), bf16[8,2,4096]{2,1,0:T(2,128)(2,1)S(1)}, u32[]{:S(2)}, u32[]{:S(2)}) async-start(bf16[8,2,4096]{2,1,0:T(2,128)(2,1)} %reshape.393), calls=%async_computation.1 | async-start | bytes 262144 | tf_op jit(solution)/shard_map/all_to_all | solution.py:84
  213.8 43.0 %reduce-scatter.2.cloned.1.call-done = f32[1024,1,128]{2,1,0:T(1,128)} async-done(((f32[8192,1,128]{2,1,0:T(1,128)}), f32[1024,1,128]{2,1,0:T(1,128)}) %reduce-scatter.2.cloned.1.call-update) | async-done | bytes 524304 | tf_op jit(solution)/shard_map/reduce_scatter | solution.py:145
  258.2 2.0 pad_maximum_fusion.1
  260.2 4.1 reduce.10
  265.6 5.7 %all-to-all-start.3 = ((bf16[8,2,12288]{2,1,0:T(2,128)(2,1)}), bf16[8,2,12288]{2,1,0:T(2,128)(2,1)S(1)}, u32[]{:S(2)}, u32[]{:S(2)}) async-start(bf16[8,2,12288]{2,1,0:T(2,128)(2,1)} %reshape.395), calls=%async_computation.4 | async-start | bytes 786432 | tf_op jit(solution)/shard_map/all_to_all | solution.py:152
  273.3 4.7 all-to-all-done.3
  279.5 2.3 fusion.38
  285.3 263.5 %all-reduce.3.cloned.1.call-done = (f32[512,1536]{0,1:T(8,128)}, f32[512,512]{0,1:T(8,128)}) async-done(((f32[512,1536]{0,1:T(8,128)}, f32[512,512]{0,1:T(8,128)}), (f32[512,1536]{0,1:T(8,128)}, f32[512,512]{0,1:T(8,128)})) %all-reduce.3.cloned.1.call-update) | async-done | bytes 4194320 | tf_op jit(solution)/shard_map/psum | solution.py:160
  548.8 1.8 constant_dynamic-slice_fusion.1
  550.6 1.6 dynamic-slice_bitcast_fusion.4
  (200 shorter events, 52.6 us)
Async XLA Ops:
  7.2 1.8 copy-start
  7.2 60.2 %all-gather.2.cloned.1.call-start = ((), (), s32[]{:S(2)}) async-start(), calls=%async_computation.5 | async-start | bytes 2359296 | tf_op jit(solution)/shard_map/all_gather | solution.py:61
  9.0 15.1 %copy-start.6 = (bf16[512,512]{1,0:T(8,128)(2,1)S(1)}, bf16[512,512]{1,0:T(8,128)(2,1)}, u32[]{:S(2)}) copy-start(bf16[512,512]{1,0:T(8,128)(2,1)} %param.19) | copy-start | bytes 1572868
  9.0 15.1 %copy-start.17 = (bf16[1,128,512]{2,1,0:T(8,128)(2,1)S(1)}, bf16[1,128,512]{2,1,0:T(8,128)(2,1)}, u32[]{:S(2)}) copy-start(bf16[1,128,512]{2,1,0:T(8,128)(2,1)} %param.21) | copy-start | bytes 393220
  10.3 19.6 %copy-start.25 = (s32[1,64,9]{1,0,2:T(1,128)S(1)}, s32[1,64,9]{1,0,2:T(1,128)}, u32[]{:S(2)}) copy-start(s32[1,64,9]{1,0,2:T(1,128)} %param.17) | copy-start | bytes 6916
  10.4 19.8 %copy-start.28 = (f32[8]{0:T(128)S(1)}, f32[8]{0:T(128)}, u32[]{:S(2)}) copy-start(f32[8]{0:T(128)} %param.20) | copy-start | bytes 100
  10.4 20.4 %copy-start.3 = (s32[1,8192]{1,0:T(1,128)S(1)}, s32[1,8192]{1,0:T(1,128)}, u32[]{:S(2)}) copy-start(s32[1,8192]{1,0:T(1,128)} %param.16) | copy-start | bytes 98308
  25.1 87.3 %all-to-all-start.2 = ((bf16[128,8,64]{0,2,1:T(8,128)(2,1)}), bf16[128,8,64]{0,2,1:T(8,128)(2,1)S(1)}, u32[]{:S(2)}, u32[]{:S(2)}) async-start(bf16[128,8,64]{0,2,1:T(8,128)(2,1)} %bitcast.50), calls=%async_computation.2 | async-start | bytes 262144 | tf_op jit(solution)/shard_map/all_to_all | solution.py:90
  29.9 226.8 %reduce-scatter.2.cloned.1.call-start = ((), (), s32[]{:S(2)}) async-start(), calls=%async_computation.6 | async-start | bytes 4718592 | tf_op jit(solution)/shard_map/reduce_scatter | solution.py:145
  78.8 1.0 copy-start.4
  79.8 0.8 copy-start.19
  80.7 5.4 copy-start.22
  84.3 1.4 copy-start.2
  86.1 3.2 copy-start.23
  86.1 3.1 copy-start.10
  98.9 1.0 copy-start.4
  100.0 0.8 copy-start.19
  100.8 5.4 copy-start.22
  104.5 1.4 copy-start.2
  106.3 3.2 copy-start.23
  106.3 3.1 copy-start.10
  116.5 2.6 copy-start.20
  116.5 6.5 %copy-start.8 = (bf16[2,4,128,1,64]{2,4,1,3,0:T(8,128)(2,1)}, bf16[2,4,128,1,64]{2,4,1,3,0:T(8,128)(2,1)S(1)}, u32[]{:S(2)}) copy-start(bf16[2,4,128,1,64]{2,4,1,3,0:T(8,128)(2,1)S(1)} %get-tuple-element.496) | copy-start | bytes 393220 | tf_op jit(solution)/shard_map/while
  140.3 2.5 copy-start.1
  142.8 1.1 copy-start.5
  142.9 1.1 copy-start.14
  142.9 1.6 copy-start.9
  144.5 1.9 copy-start.15
  146.5 3.1 copy-start.24
  149.6 10.0 %copy-start.21 = (f32[2,4,1,128]{3,1,2,0:T(4,128)S(1)}, f32[2,4,1,128]{3,1,2,0:T(4,128)}, u32[]{:S(2)}) copy-start(f32[2,4,1,128]{3,1,2,0:T(4,128)} %copy-done.20) | copy-start | bytes 12292 | tf_op jit(solution)/shard_map/while
  159.5 2.6 copy-start.20
  159.5 6.5 %copy-start.8 = (bf16[2,4,128,1,64]{2,4,1,3,0:T(8,128)(2,1)}, bf16[2,4,128,1,64]{2,4,1,3,0:T(8,128)(2,1)S(1)}, u32[]{:S(2)}) copy-start(bf16[2,4,128,1,64]{2,4,1,3,0:T(8,128)(2,1)S(1)} %get-tuple-element.496) | copy-start | bytes 393220 | tf_op jit(solution)/shard_map/while
  183.3 2.5 copy-start.1
  185.8 1.1 copy-start.5
  185.8 1.1 copy-start.14
  185.8 1.6 copy-start.9
  187.5 1.9 copy-start.15
  189.4 3.1 copy-start.24
  192.5 10.0 %copy-start.21 = (f32[2,4,1,128]{3,1,2,0:T(4,128)S(1)}, f32[2,4,1,128]{3,1,2,0:T(4,128)}, u32[]{:S(2)}) copy-start(f32[2,4,1,128]{3,1,2,0:T(4,128)} %copy-done.20) | copy-start | bytes 12292 | tf_op jit(solution)/shard_map/while
  202.6 0.9 copy-start.12
  203.5 9.9 %copy-start.16 = (bf16[2,4,128,1,64]{2,4,1,3,0:T(8,128)(2,1)S(1)}, bf16[2,4,128,1,64]{2,4,1,3,0:T(8,128)(2,1)}, u32[]{:S(2)}) copy-start(bf16[2,4,128,1,64]{2,4,1,3,0:T(8,128)(2,1)} %get-tuple-element.119) | copy-start | bytes 393220
  207.7 57.9 %all-to-all-start.1 = ((bf16[8,2,4096]{2,1,0:T(2,128)(2,1)}), bf16[8,2,4096]{2,1,0:T(2,128)(2,1)S(1)}, u32[]{:S(2)}, u32[]{:S(2)}) async-start(bf16[8,2,4096]{2,1,0:T(2,128)(2,1)} %reshape.393), calls=%async_computation.1 | async-start | bytes 262144 | tf_op jit(solution)/shard_map/all_to_all | solution.py:84
  260.2 11.9 %copy-start.18 = (bf16[1,128,512]{2,1,0:T(8,128)(2,1)S(1)}, bf16[1,128,512]{2,1,0:T(8,128)(2,1)}, u32[]{:S(2)}) copy-start(bf16[1,128,512]{2,1,0:T(8,128)(2,1)} %param.21) | copy-start | bytes 393220
  265.6 12.4 %all-to-all-start.3 = ((bf16[8,2,12288]{2,1,0:T(2,128)(2,1)}), bf16[8,2,12288]{2,1,0:T(2,128)(2,1)S(1)}, u32[]{:S(2)}, u32[]{:S(2)}) async-start(bf16[8,2,12288]{2,1,0:T(2,128)(2,1)} %reshape.395), calls=%async_computation.4 | async-start | bytes 786432 | tf_op jit(solution)/shard_map/all_to_all | solution.py:152
  271.3 277.5 %all-reduce.3.cloned.1.call-start = ((), (), s32[]{:S(2)}) async-start(), calls=%async_computation.7 | async-start | bytes 8388608 | tf_op jit(solution)/shard_map/psum | solution.py:160
  273.3 6.2 %copy-start.13 = (bf16[1,128,512]{2,1,0:T(8,128)(2,1)S(1)}, bf16[1,128,512]{2,1,0:T(8,128)(2,1)}, u32[]{:S(2)}) copy-start(bf16[1,128,512]{2,1,0:T(8,128)(2,1)} %param.15) | copy-start | bytes 393220
  273.3 6.2 %copy-start.27 = (f32[128]{0:T(128)S(1)}, f32[128]{0:T(128)}, u32[]{:S(2)}) copy-start(f32[128]{0:T(128)} %copy-done.26) | copy-start | bytes 1540
  281.8 1.0 copy-start.7
  (3 other events, 1.9 us)
Sparse Core Ops, SparseCore 0:
  24.2 43.1 all-gather.1
  202.7 53.9 reduce-scatter.1
  281.9 266.7 all-reduce.2
where the time goes:
time: 561 us; the launch traced here: 559 us
  waiting for transfers between devices  348 us (62%)
  local copies, waits for them, and re-layouts  90.9 us (16%)
  other arithmetic  41.3 us (7%)
  matrix products  35.3 us (6%)
  starting transfers between devices  16.3 us (3%)
  between operations  14 us (2%)
  blocking collectives  12.6 us (2%)
    psum x1, waiting for transfers between devices, body(): lax.psum((local_qkv, local_out), ('dp', 'seq', 'head'))  264 us
    reduce_scatter x1, waiting for transfers between devices, body(): lax.psum_scatter(pair_sums.reshape(seq_length, local_heads, 2 * HD), 'seq...  43 us
    all_gather x1, waiting for transfers between devices, body(): pair_all = lax.all_gather(pair_local, 'seq', axis=0, tiled=True)  36.5 us
    scatter-add x2, other arithmetic, scatter_step(): carried = carried.at[key_rows.reshape(-1)].add(both_parts)  20 us
    dot_general x4, matrix products, query_scores(): jnp.einsum('gqhe,gnkhe->ghqnk', query_blk, key_blk, preferred_element_typ...  15.7 us
    all_to_all x1, blocking collectives, body(): lax.all_to_all(packed, 'head', split_axis=1, concat_axis=0, tiled=True)  12.6 us
    reshape x4, local copies, waits for them, and re-layouts, query_scores(): return scores.reshape(scores.shape[0], scores.shape[1], scores.shape[2], -1)  12.5 us
  transfers between devices with their start and end apart: 6, of which 4 were waited for; matrix products, arithmetic and copies ran while one was open for 10% of the time, Pallas kernels for 0%

commit v1 on v0

--- a/solution.py
+++ b/solution.py
@@ -157,7 +157,7 @@
     grad_input = ((grad_hidden - normed * inner) / spread).astype(jnp.bfloat16)
     local_qkv = jnp.einsum("td,tc->dc", hidden, grad_packed, preferred_element_type=jnp.float32)
     local_out = jnp.einsum("td,tc->dc", grad_rows, attended_tok, preferred_element_type=jnp.float32)
-    total_qkv, total_out = lax.psum((local_qkv, local_out), ("dp", "seq", "head"))
+    total_qkv, total_out = lax.psum(lax.psum((local_qkv, local_out), ("seq", "head")), "dp")
     own_qkv = lax.dynamic_slice_in_dim(
         total_qkv, head_pos * local_heads * 3 * HD, local_heads * 3 * HD, 1
     )

time: 561 us -> 1010 us (1.80)
  waiting for transfers between devices: 348 us -> 798 us
    psum x1 -> x2, waiting for transfers between devices: 264 us -> 714 us  [the longest x1 618 us: body(): lax.psum((local_qkv, local_out), ('seq', 'head'))]
  transfers between devices with their start and end apart: 6 -> 7, of which waited for: 4 -> 5; matrix products, arithmetic and copies ran while one was open for 10% -> 6% of each run, Pallas kernels for 0% -> 0%
where the time goes in v1:
time: 1010 us
  waiting for transfers between devices  798 us (79%)
  local copies, waits for them, and re-layouts  90 us (9%)
  other arithmetic  41.3 us (4%)
  matrix products  35.5 us (4%)
  starting transfers between devices  16.3 us (2%)
  between operations  14.1 us (1%)
  blocking collectives  12.6 us (1%)
    psum x1, waiting for transfers between devices, body(): lax.psum((local_qkv, local_out), ('seq', 'head'))  618 us
    psum x1, waiting for transfers between devices, body(): lax.psum(lax.psum((local_qkv, local_out), ('seq', 'head')), 'dp')  96.4 us
    reduce_scatter x1, waiting for transfers between devices, body(): lax.psum_scatter(pair_sums.reshape(seq_length, local_heads, 2 * HD), 'seq...  43.1 us
    all_gather x1, waiting for transfers between devices, body(): pair_all = lax.all_gather(pair_local, 'seq', axis=0, tiled=True)  36.5 us
  transfers between devices with their start and end apart: 7, of which 5 were waited for; matrix products, arithmetic and copies ran while one was open for 6% of the time, Pallas kernels for 0%

profile of v1, /device:TPU:2, one launch (start us, length us, event | category | flops | bytes accessed | tf_op | source)
XLA Modules:
  0.0 1008.5 jit_solution(12251053179627305069)
XLA Ops:
  10.6 12.6 %all_to_all.63 = bf16[128,8,192]{0,2,1:T(8,128)(2,1)S(1)} all-to-all(bf16[128,8,192]{0,2,1:T(8,128)(2,1)S(1)} %bitcast.271), channel_id=1, replica_groups=mesh['dp'=4,'seq'=8,'head'=8] {'head'}, dimensions={1} | all-to-all | bytes 786432 | tf_op jit(solution)/shard_map/all_to_all | solution.py:58
  25.1 4.8 all-to-all-start.2
  30.9 36.5 %all-gather.2.cloned.1.call-done = bf16[8192,1,128]{0,2,1:T(8,128)(2,1)} async-done(((bf16[1024,1,128]{0,2,1:T(8,128)(2,1)}), bf16[8192,1,128]{0,2,1:T(8,128)(2,1)}) %all-gather.2.cloned.1.call-update) | async-done | bytes 2097168 | tf_op jit(solution)/shard_map/all_gather | solution.py:61
  67.4 4.1 copy.119
  72.1 40.4 %while.24 = (s32[]{:T(128)}, bf16[2,4,128,1,64]{2,4,1,3,0:T(8,128)(2,1)}, f32[2,4,1,128]{3,1,2,0:T(4,128)}, s32[2,4,9]{2,1,0:T(4,128)S(1)}, bf16[64,128,1,128]{3...) while((s32[]{:T(128)}, ...), condition=%wide.region_4.7_spmd, body=%wide.region_1.6_spmd.sunk | while | flops 156931296 | bytes 39141280 | solution.py:79
  73.5 3.4 gather_fusion
  76.9 1.7 copy.151
  80.7 3.7 fusion.80
  86.2 3.1 copy.153
  89.3 2.3 fusion.81
  93.7 3.4 gather_fusion
  97.1 1.7 copy.151
  100.9 3.7 fusion.80
  106.4 3.1 copy.153
  109.5 2.3 fusion.81
  114.1 2.5 broadcast_in_dim.54
  116.6 86.2 %while.25 = (s32[]{:T(128)}, f32[64,128,1,128]{3,1,0,2:T(8,128)}, bf16[2,4,128,1,64]{2,4,1,3,0:T(8,128)(2,1)}, s32[2,4,9]{2,1,0:T(4,128)S(1)}, bf16[2,4,128,1,64...) while((s32[]{:T(128)}, f32[64,128,1,128]{3,1,0,2:T(8,128)}, ...), condition=%wide.region_8.11_spmd, body=%wide.region_6.10_spmd.sunk | while | flops 385783744 | bytes 64560684 | solution.py:144
  119.2 2.4 gather_fusion.3
  126.9 1.5 reshape.431
  128.4 2.5 copy.158
  130.9 2.1 reshape.432
  133.0 4.2 select_add_fusion.3
  137.2 3.1 copy.155
  140.3 2.5 fusion.94
  144.9 1.6 pad_maximum_fusion.3
  146.5 3.1 copy.157
  149.6 10.1 scatter_fusion
  162.3 2.4 gather_fusion.3
  171.4 2.5 copy.158
  173.9 2.1 reshape.432
  176.1 4.2 select_add_fusion.3
  180.3 3.1 copy.155
  183.4 2.5 fusion.94
  187.9 1.6 pad_maximum_fusion.3
  189.6 3.1 copy.157
  192.7 10.1 scatter_fusion
  204.7 2.3 reduce.9
  207.9 5.7 all-to-all-start.1
  213.9 43.1 %reduce-scatter.2.cloned.1.call-done = f32[1024,1,128]{2,1,0:T(1,128)} async-done(((f32[8192,1,128]{2,1,0:T(1,128)}), f32[1024,1,128]{2,1,0:T(1,128)}) %reduce-scatter.2.cloned.1.call-update) | async-done | bytes 524304 | tf_op jit(solution)/shard_map/reduce_scatter | solution.py:145
  258.4 2.0 pad_maximum_fusion.1
  260.4 4.1 reduce.10
  265.8 5.7 all-to-all-start.3
  273.6 4.6 all-to-all-done.3
  279.7 2.3 fusion.38
  282.1 617.6 %all-reduce.5.cloned.1.call-done = (f32[512,1536]{0,1:T(8,128)}, f32[512,512]{0,1:T(8,128)}) async-done(((f32[512,1536]{0,1:T(8,128)}, f32[512,512]{0,1:T(8,128)}), (f32[512,1536]{0,1:T(8,128)}, f32[512,512]{0,1:T(8,128)})) %all-reduce.5.cloned.1.call-update) | async-done | bytes 4194320 | tf_op jit(solution)/shard_map/psum | solution.py:160
  902.2 96.4 %all-reduce.7.cloned.1.call-done = (f32[512,1536]{0,1:T(8,128)}, f32[512,512]{0,1:T(8,128)}) async-done(((f32[512,1536]{0,1:T(8,128)}, f32[512,512]{0,1:T(8,128)}), (f32[512,1536]{0,1:T(8,128)}, f32[512,512]{0,1:T(8,128)})) %all-reduce.7.cloned.1.call-update) | async-done | bytes 4194320 | tf_op jit(solution)/shard_map/psum | solution.py:160
  998.7 1.8 constant_dynamic-slice_fusion.1
  1000.4 1.6 dynamic-slice_bitcast_fusion.4
  (203 shorter events, 53.1 us)
Async XLA Ops:
  7.2 1.8 copy-start
  7.2 60.2 %all-gather.2.cloned.1.call-start = ((), (), s32[]{:S(2)}) async-start(), calls=%async_computation.5 | async-start | bytes 2359296 | tf_op jit(solution)/shard_map/all_gather | solution.py:61
  9.0 15.1 %copy-start.6 = (bf16[512,512]{1,0:T(8,128)(2,1)S(1)}, bf16[512,512]{1,0:T(8,128)(2,1)}, u32[]{:S(2)}) copy-start(bf16[512,512]{1,0:T(8,128)(2,1)} %param.19) | copy-start | bytes 1572868
  9.0 15.1 %copy-start.17 = (bf16[1,128,512]{2,1,0:T(8,128)(2,1)S(1)}, bf16[1,128,512]{2,1,0:T(8,128)(2,1)}, u32[]{:S(2)}) copy-start(bf16[1,128,512]{2,1,0:T(8,128)(2,1)} %param.21) | copy-start | bytes 393220
  10.3 19.6 %copy-start.25 = (s32[1,64,9]{1,0,2:T(1,128)S(1)}, s32[1,64,9]{1,0,2:T(1,128)}, u32[]{:S(2)}) copy-start(s32[1,64,9]{1,0,2:T(1,128)} %param.17) | copy-start | bytes 6916
  10.4 19.8 %copy-start.28 = (f32[8]{0:T(128)S(1)}, f32[8]{0:T(128)}, u32[]{:S(2)}) copy-start(f32[8]{0:T(128)} %param.20) | copy-start | bytes 100
  10.4 20.4 %copy-start.3 = (s32[1,8192]{1,0:T(1,128)S(1)}, s32[1,8192]{1,0:T(1,128)}, u32[]{:S(2)}) copy-start(s32[1,8192]{1,0:T(1,128)} %param.16) | copy-start | bytes 98308
  25.1 87.4 %all-to-all-start.2 = ((bf16[128,8,64]{0,2,1:T(8,128)(2,1)}), bf16[128,8,64]{0,2,1:T(8,128)(2,1)S(1)}, u32[]{:S(2)}, u32[]{:S(2)}) async-start(bf16[128,8,64]{0,2,1:T(8,128)(2,1)} %bitcast.50), calls=%async_computation.2 | async-start | bytes 262144 | tf_op jit(solution)/shard_map/all_to_all | solution.py:90
  29.9 227.0 %reduce-scatter.2.cloned.1.call-start = ((), (), s32[]{:S(2)}) async-start(), calls=%async_computation.6 | async-start | bytes 4718592 | tf_op jit(solution)/shard_map/reduce_scatter | solution.py:145
  78.8 1.0 copy-start.4
  79.8 0.8 copy-start.19
  80.7 5.5 copy-start.22
  84.4 1.4 copy-start.2
  86.2 3.1 copy-start.23
  86.2 3.1 copy-start.10
  99.0 1.0 copy-start.4
  100.9 5.5 copy-start.22
  104.6 1.4 copy-start.2
  106.4 3.1 copy-start.23
  106.4 3.1 copy-start.10
  116.6 2.6 copy-start.20
  116.6 6.5 copy-start.8
  140.3 2.5 copy-start.1
  142.9 1.1 copy-start.5
  142.9 1.1 copy-start.14
  142.9 1.6 copy-start.9
  144.6 1.9 copy-start.15
  146.5 3.1 copy-start.24
  149.6 10.1 %copy-start.21 = (f32[2,4,1,128]{3,1,2,0:T(4,128)S(1)}, f32[2,4,1,128]{3,1,2,0:T(4,128)}, u32[]{:S(2)}) copy-start(f32[2,4,1,128]{3,1,2,0:T(4,128)} %copy-done.20) | copy-start | bytes 12292 | tf_op jit(solution)/shard_map/while
  159.7 2.5 copy-start.20
  159.7 6.4 copy-start.8
  183.4 2.5 copy-start.1
  185.9 1.1 copy-start.5
  186.0 1.1 copy-start.14
  186.0 1.6 copy-start.9
  187.6 1.9 copy-start.15
  189.6 3.1 copy-start.24
  192.7 10.1 copy-start.21
  202.7 0.9 copy-start.12
  203.7 9.9 copy-start.16
  207.9 57.9 %all-to-all-start.1 = ((bf16[8,2,4096]{2,1,0:T(2,128)(2,1)}), bf16[8,2,4096]{2,1,0:T(2,128)(2,1)S(1)}, u32[]{:S(2)}, u32[]{:S(2)}) async-start(bf16[8,2,4096]{2,1,0:T(2,128)(2,1)} %reshape.393), calls=%async_computation.1 | async-start | bytes 262144 | tf_op jit(solution)/shard_map/all_to_all | solution.py:84
  260.4 11.9 %copy-start.18 = (bf16[1,128,512]{2,1,0:T(8,128)(2,1)S(1)}, bf16[1,128,512]{2,1,0:T(8,128)(2,1)}, u32[]{:S(2)}) copy-start(bf16[1,128,512]{2,1,0:T(8,128)(2,1)} %param.21) | copy-start | bytes 393220
  265.8 12.4 %all-to-all-start.3 = ((bf16[8,2,12288]{2,1,0:T(2,128)(2,1)}), bf16[8,2,12288]{2,1,0:T(2,128)(2,1)S(1)}, u32[]{:S(2)}, u32[]{:S(2)}) async-start(bf16[8,2,12288]{2,1,0:T(2,128)(2,1)} %reshape.395), calls=%async_computation.4 | async-start | bytes 786432 | tf_op jit(solution)/shard_map/all_to_all | solution.py:152
  271.5 628.2 %all-reduce.5.cloned.1.call-start = ((), (), s32[]{:S(2)}) async-start(), calls=%async_computation.7 | async-start | bytes 8388608 | tf_op jit(solution)/shard_map/psum | solution.py:160
  273.6 6.1 copy-start.13
  273.6 6.1 copy-start.27
  282.1 617.7 %copy-start.7 = (bf16[512,512]{1,0:T(8,128)(2,1)S(1)}, bf16[512,512]{1,0:T(8,128)(2,1)}, u32[]{:S(2)}) copy-start(bf16[512,512]{1,0:T(8,128)(2,1)} %param.19) | copy-start | bytes 1572868
  282.1 716.6 %all-reduce.7.cloned.1.call-start = ((), (), s32[]{:S(2)}) async-start(), calls=%async_computation.8 | async-start | bytes 8388608 | tf_op jit(solution)/shard_map/psum | solution.py:160
  (4 other events, 2.7 us)
Sparse Core Ops, SparseCore 0:
  24.2 43.1 all-gather.1
  202.9 54.0 reduce-scatter.1
  282.2 617.5 all-reduce.4
  902.6 96.0 all-reduce.6
